TPU v7x, 256 devices: a whole 4x4x8 slice. The times are simulated.
256 devices in a mesh: srv: 2 (over core), smp: 128 (over y, z, x).
Axes of the slice: x: 4, y: 4, z: 8, core: 2. Of those that a mesh axis runs over, the one named last changes fastest.
Arguments:
- genotype_sites: float32 [2, 1024, 32768], P('srv', None, 'smp'), may hold values from -6 to 8, as said below
- covariate_sites: float32 [2, 10, 32768], P('srv', None, 'smp'), may hold values from -8 to 10
- sample_ids: int32 [32768], P('smp'), may hold values from -1 to 16383, as said below
- mask_cov_first: float32 [2, 10, 16384], P('srv', None, 'smp'), may hold values from -6 to 6
- mask_geno: float32 [2, 1024, 16384], P('srv', None, 'smp'), may hold values from -6 to 6
- prod_first: float32 [2, 10, 1024], P('srv'), as said below
- mask_cov_second: float32 [2, 10, 16384], P('srv', None, 'smp'), may hold values from -6 to 6
- mask_weight: float32 [2, 10, 1024], P('srv'), may hold values from -6 to 6
- prod_second: float32 [2, 1024, 16384], P('srv', None, 'smp'), as said below
- coef: float32 [10, 10], replicated
- phenotypes: float32 [16384, 32], P('smp'), may hold values from -6 to 6
Outputs:
- residual_share: float32 [2, 1024, 16384], P('srv', 'smp')
- score_share: float32 [2, 1024, 32], P('srv', 'smp')
Inputs may be any that keep to these rules, and one draw needn't show every extreme that they name: `sample_ids`: every individual 0 to 16383 is named exactly once, all other entries are -1. Individual i belongs to sample block i // 128. Of the 256 entries of one device at most 2 belong to one sample block, and every block has a device with exactly 2 of them. `genotype_sites`: the two servers' shares add up to genotypes 0, 1 or 2. `prod_first`: the two shares add up to the product of the summed covariate mask and the summed genotype mask over all individuals. `prod_second`: the two shares add up to the summed coefficient mask transposed times the summed covariate mask.
All inputs are finite; a program needn't handle non-finite values.
Results may differ from a plain program's by a relative error of at most 0.0001.
Values sent between devices are 32-bit elements; how exact they have to be, the bound alone decides.
No kernel may reach another device: no remote copies, remote signals or barrier semaphores. Data moves between devices by JAX's collectives and lax.ppermute only.
A program may use at most 64 MiB of HBM per device.

v0:
```python
import math
import jax
import jax.numpy as jnp
from jax import lax
from jax.sharding import PartitionSpec as P

ROWS = 128
precise = lax.Precision.HIGHEST


def from_partner(value, axis, apart):
    mask = 2**apart
    pairs = [(source, source ^ mask) for source in range(lax.axis_size(axis))]
    return lax.ppermute(value, axis, pairs)


def contract_last(left, right):
    return lax.dot_general(
        left, right, (((1,), (1,)), ((), ())), precision=precise, preferred_element_type=jnp.float32
    )


def contract_first(left, right):
    return lax.dot_general(
        left, right, (((0,), (0,)), ((), ())), precision=precise, preferred_element_type=jnp.float32
    )


def pack_columns(site_geno, site_cov, sample_ids, block_count):
    capacity = sample_ids.shape[0]
    slot_width = capacity // block_count
    is_live = sample_ids >= 0
    owner_block = jnp.where(is_live, sample_ids // ROWS, 0)
    membership = (
        (owner_block[:, None] == jnp.arange(block_count, dtype=jnp.int32)[None, :])
        & is_live[:, None]
    ).astype(jnp.int32)
    earlier_count = jnp.cumsum(membership, axis=0) - membership
    rank_within = jnp.sum(earlier_count * membership, axis=1)
    slot_index = jnp.where(is_live, owner_block * slot_width + rank_within, capacity)
    source_column = (
        jnp.zeros((capacity,), jnp.int32)
        .at[slot_index]
        .set(jnp.arange(capacity, dtype=jnp.int32), mode="drop")
    )
    slot_used = jnp.zeros((capacity,), jnp.float32).at[slot_index].set(1.0, mode="drop")
    local_row = jnp.where(is_live, sample_ids % ROWS, -1).astype(jnp.float32)
    placed_row = jnp.where(slot_used > 0, local_row[source_column], -1.0)
    packed_geno = jnp.take(site_geno, source_column, axis=1) * slot_used[None, :]
    packed_cov = jnp.take(site_cov, source_column, axis=1) * slot_used[None, :]
    return (packed_geno, packed_cov, placed_row[None, :])


def local(
    genotype_sites,
    covariate_sites,
    sample_ids,
    mask_cov_first,
    mask_geno,
    prod_first,
    mask_cov_second,
    mask_weight,
    prod_second,
    coef,
    phenotypes,
):
    block_count = lax.axis_size("smp")
    leader = (lax.axis_index("srv") == 0).astype(jnp.float32)
    packed_geno, packed_cov, placed_row = pack_columns(
        genotype_sites[0], covariate_sites[0], sample_ids, block_count
    )
    recv_geno, recv_cov, recv_row = (
        lax.all_to_all(packed_geno, "smp", split_axis=1, concat_axis=1, tiled=True),
        lax.all_to_all(packed_cov, "smp", split_axis=1, concat_axis=1, tiled=True),
        lax.all_to_all(placed_row, "smp", split_axis=1, concat_axis=1, tiled=True),
    )
    target = jnp.where(recv_row[0] >= 0, recv_row[0], float(ROWS)).astype(jnp.int32)
    block_geno = (
        jnp.zeros((recv_geno.shape[0], ROWS), jnp.float32).at[:, target].set(recv_geno, mode="drop")
    )
    block_cov = (
        jnp.zeros((recv_cov.shape[0], ROWS), jnp.float32).at[:, target].set(recv_cov, mode="drop")
    )
    masked_cov = block_cov - mask_cov_first[0]
    masked_geno = block_geno - mask_geno[0]
    masked_second = block_cov - mask_cov_second[0]
    peer_cov, peer_geno = from_partner((masked_cov, masked_geno), "srv", 0)
    open_cov = masked_cov + peer_cov
    open_geno = masked_geno + peer_geno
    partial_value = (
        contract_last(open_cov, mask_geno[0])
        + contract_last(mask_cov_first[0], open_geno)
        + leader * contract_last(open_cov, open_geno)
    )
    gram_share = prod_first[0] + lax.psum(partial_value, "smp")
    weight_share = jnp.dot(coef, gram_share, precision=precise, preferred_element_type=jnp.float32)
    masked_weight = weight_share - mask_weight[0]
    peer_second, peer_weight = from_partner((masked_second, masked_weight), "srv", 0)
    open_second = masked_second + peer_second
    open_weight = masked_weight + peer_weight
    fitted = (
        prod_second[0]
        + contract_first(mask_weight[0], open_second)
        + contract_first(open_weight, mask_cov_second[0])
        + leader * contract_first(open_weight, open_second)
    )
    residual = block_geno - fitted
    columns = lax.all_to_all(residual, "smp", split_axis=0, concat_axis=1, tiled=True)
    scale = 1.0 / math.sqrt(ROWS * block_count)
    scores = jnp.dot(
        columns,
        lax.all_gather(phenotypes, "smp", axis=0, tiled=True),
        precision=precise,
        preferred_element_type=jnp.float32,
    )
    return (columns[None], (scores * scale)[None])


def solution(mesh):
    return jax.shard_map(
        local,
        mesh=mesh,
        in_specs=(
            P("srv", None, "smp"),
            P("srv", None, "smp"),
            P("smp"),
            P("srv", None, "smp"),
            P("srv", None, "smp"),
            P("srv", None, None),
            P("srv", None, "smp"),
            P("srv", None, None),
            P("srv", None, "smp"),
            P(),
            P("smp", None),
        ),
        out_specs=(P("srv", "smp", None), P("srv", "smp", None)),
        check_vma=False,
    )
```

profile of v0, /device:TPU:32, one launch (start us, length us, event | category | flops | bytes accessed | tf_op | source)
XLA Modules:
  0.0 829.3 jit_solution(5428320511166354375)
XLA Ops:
  7.2 0.8 fusion.38
  8.1 0.1 copy.35
  8.2 0.3 fusion.14
  8.7 0.2 fusion.16
  8.9 0.7 compare_select_fusion.3
  9.6 1.4 scatter_custom_fusion.1
  11.0 1.4 scatter_custom_fusion
  12.4 1.9 gather_fusion
  14.4 0.8 all_to_all.32
  15.1 15.0 %all-to-all-start = ((f32[1,128,2]{2,0,1:T(1,128)}), f32[1,128,2]{2,0,1:T(1,128)S(1)}, u32[]{:S(2)}, u32[]{:S(2)}) async-start(f32[1,128,2]{2,0,1:T(1,128)} %bitcast.5), calls=%async_computation | async-start | bytes 131072 | tf_op jit(solution)/shard_map/all_to_all | solution.py:75
  30.2 0.1 mul.50
  30.3 0.3 copy.38
  30.7 1.1 gather_fusion.1
  31.7 0.6 gather.17
  32.4 0.2 broadcast_in_dim.72
  32.5 1.6 select_multiply_fusion
  34.1 7.2 all-to-all-done
  41.3 6.6 all-to-all-start.1
  48.0 0.7 all-gather.2.cloned.1.call-update
  48.7 0.2 copy.43
  48.9 0.5 broadcast.135
  49.4 0.8 reduce.3
  50.2 0.1 squeeze.32
  50.4 27.2 %all-to-all-done.1 = f32[1024,128,2]{0,2,1:T(2,128)S(1)} async-done(((f32[1024,128,2]{0,2,1:T(2,128)}), f32[1024,128,2]{0,2,1:T(2,128)S(1)}, u32[]{:S(2)}, u32[]{:S(2)}) %all-to-all-start.1) | async-done | bytes 1048608 | tf_op jit(solution)/shard_map/all_to_all | solution.py:73
  77.6 0.7 reshape.136
  78.3 1.6 scatter_custom_fusion.2
  80.0 0.3 collective-permute-start.2
  80.4 0.7 gather_fusion.2
  81.2 1.0 select_multiply_fusion.1
  82.2 7.2 all-to-all-start.2
  89.6 12.0 %all-to-all-done.2 = f32[10,128,2]{0,2,1:T(2,128)S(1)} async-done(((f32[10,128,2]{0,2,1:T(2,128)}), f32[10,128,2]{0,2,1:T(2,128)S(1)}, u32[]{:S(2)}, u32[]{:S(2)}) %all-to-all-start.2) | async-done | bytes 10272 | tf_op jit(solution)/shard_map/all_to_all | solution.py:74
  101.6 1.2 scatter_custom_fusion.3
  103.0 0.4 convolution_bitcast_fusion.2
  103.4 0.8 collective-permute-done.1
  104.2 0.4 convolution_multiply_fusion.1
  104.6 0.6 fusion.5
  105.1 673.8 %psum.7 = f32[10,1024]{1,0:T(8,128)S(1)} all-reduce(f32[10,1024]{1,0:T(8,128)S(1)} %fusion.5), channel_id=1, replica_groups=mesh['srv'=2,'smp'=128] {'smp'}, use_global_device_ids=true, to_apply=%region_7.8 | all-reduce | flops 10240 | bytes 81920 | tf_op jit(solution)/shard_map/psum | solution.py:95
  778.9 0.2 fusion.4
  779.2 0.2 copy.39
  779.4 0.6 collective-permute-start
  780.0 0.5 collective-permute-done.3
  780.5 0.6 fusion.24
  781.0 0.6 convolution_multiply_fusion
  781.6 0.7 fusion.3
  782.3 0.2 copy.46
  782.5 35.2 %all_to_all.46 = f32[128,8,128]{2,1,0:T(8,128)S(1)} all-to-all(f32[128,8,128]{2,1,0:T(8,128)S(1)} %bitcast.87), channel_id=1, replica_groups=mesh['srv'=2,'smp'=128] {'smp'}, dimensions={0} | all-to-all | bytes 1048576 | tf_op jit(solution)/shard_map/all_to_all | solution.py:108
  817.7 4.0 fusion.6
  821.7 0.8 copy.61
  (43 shorter events, 0.9 us)
Async XLA Ops:
  7.2 771.7 %copy-start = (f32[10,10]{1,0:T(8,128)S(1)}, f32[10,10]{1,0:T(8,128)}, u32[]{:S(2)}) copy-start(f32[10,10]{1,0:T(8,128)} %param.20) | copy-start | bytes 1204
  7.2 23.1 %copy-start.2 = (f32[1,1024,256]{2,1,0:T(8,128)S(1)}, f32[1,1024,256]{2,1,0:T(8,128)}, u32[]{:S(2)}) copy-start(f32[1,1024,256]{2,1,0:T(8,128)} %param.11) | copy-start | bytes 3145732
  15.1 26.1 %all-to-all-start = ((f32[1,128,2]{2,0,1:T(1,128)}), f32[1,128,2]{2,0,1:T(1,128)S(1)}, u32[]{:S(2)}, u32[]{:S(2)}) async-start(f32[1,128,2]{2,0,1:T(1,128)} %bitcast.5), calls=%async_computation | async-start | bytes 131072 | tf_op jit(solution)/shard_map/all_to_all | solution.py:75
  32.5 16.2 %copy-start.1 = (f32[1,1024,128]{2,1,0:T(8,128)S(1)}, f32[1,1024,128]{2,1,0:T(8,128)}, u32[]{:S(2)}) copy-start(f32[1,1024,128]{2,1,0:T(8,128)} %param.15) | copy-start | bytes 1572868
  41.3 36.3 %all-to-all-start.1 = ((f32[1024,128,2]{0,2,1:T(2,128)}), f32[1024,128,2]{0,2,1:T(2,128)S(1)}, u32[]{:S(2)}, u32[]{:S(2)}) async-start(f32[1024,128,2]{0,2,1:T(2,128)} %select_multiply_fusion), calls=%async_computation.1 | async-start | bytes 2097152 | tf_op jit(solution)/shard_map/all_to_all | solution.py:73
  47.9 769.8 %all-gather.2.cloned.1.call-start = ((), (), s32[]{:S(2)}) async-start(), calls=%async_computation.4 | async-start | bytes 2113536 | tf_op jit(solution)/shard_map/all_gather | solution.py:112
  78.3 2.0 copy-start.6
  78.3 11.0 %copy-start.7 = (f32[1,10,128]{2,0,1:T(1,128)S(1)}, f32[1,10,128]{2,0,1:T(1,128)}, u32[]{:S(2)}) copy-start(f32[1,10,128]{2,0,1:T(1,128)} %param.14) | copy-start | bytes 15364
  78.3 11.2 %copy-start.8 = (f32[1,10,128]{2,0,1:T(1,128)S(1)}, f32[1,10,128]{2,0,1:T(1,128)}, u32[]{:S(2)}) copy-start(f32[1,10,128]{2,0,1:T(1,128)} %param.17) | copy-start | bytes 15364
  80.0 22.9 %collective-permute-start.2 = (f32[1024,128]{0,1:T(8,128)S(1)}, f32[1024,128]{0,1:T(8,128)S(1)}, u32[]{:S(2)}, u32[]{:S(2)}) collective-permute-start(f32[1024,128]{0,1:T(8,128)S(1)} %bitcast_subtract_fusion), channel_id=1, source_target_pairs={{0,128},{128,0},{1,129},{129,1},{2,130},{130,2},{3,131},{131,3},{4... | collective-permute-start | bytes 1572872 | tf_op jit(solution)/shard_map/ppermute | solution.py:14
  82.2 696.8 %copy-start.4 = (f32[1,10,1024]{2,0,1:T(1,128)S(1)}, f32[1,10,1024]{2,0,1:T(1,128)}, u32[]{:S(2)}) copy-start(f32[1,10,1024]{2,0,1:T(1,128)} %param.18) | copy-start | bytes 122884
  82.2 696.8 %copy-start.5 = (f32[1,10,1024]{2,0,1:T(1,128)S(1)}, f32[1,10,1024]{2,0,1:T(1,128)}, u32[]{:S(2)}) copy-start(f32[1,10,1024]{2,0,1:T(1,128)} %param.16) | copy-start | bytes 122884
  82.2 19.5 %all-to-all-start.2 = ((f32[10,128,2]{0,2,1:T(2,128)}), f32[10,128,2]{0,2,1:T(2,128)S(1)}, u32[]{:S(2)}, u32[]{:S(2)}) async-start(f32[10,128,2]{0,2,1:T(2,128)} %select_multiply_fusion.1), calls=%async_computation.2 | async-start | bytes 262144 | tf_op jit(solution)/shard_map/all_to_all | solution.py:74
  89.4 689.9 %copy-start.3 = (f32[1,1024,128]{2,1,0:T(8,128)S(1)}, f32[1,1024,128]{2,1,0:T(8,128)}, u32[]{:S(2)}) copy-start(f32[1,1024,128]{2,1,0:T(8,128)} %param.19) | copy-start | bytes 1572868
  102.8 1.3 collective-permute-start.1
  779.1 1.3 collective-permute-start.3
  779.4 1.6 collective-permute-start
Sparse Core Ops, SparseCore 0:
  52.2 108.3 all-gather.1
where the time goes:
time: 830 us; the launch traced here: 829 us
  blocking collectives  709 us (85%)
  waiting for transfers between devices  48.4 us (6%)
  starting transfers between devices  29.9 us (4%)
  local copies, waits for them, and re-layouts  14.7 us (2%)
  between operations  14.4 us (2%)
    psum x1, blocking collectives, local(): gram_share = prod_first[0] + lax.psum(partial_value, 'smp')  674 us
    all_to_all x1, blocking collectives, local(): lax.all_to_all(residual, 'smp', split_axis=0, concat_axis=1, tiled=True)  35.2 us
    all_to_all x1, waiting for transfers between devices, local(): lax.all_to_all(packed_geno, 'smp', split_axis=1, concat_axis=1, tiled=True)  27.2 us
  transfers between devices with their start and end apart: 8, of which 5 were waited for; matrix products, arithmetic and copies ran while one was open for 2% of the time, Pallas kernels for 0%

commit v1 on v0

--- a/solution.py
+++ b/solution.py
@@ -6,6 +6,11 @@
 
 ROWS = 128
 precise = lax.Precision.HIGHEST
+
+
+def add_all(x, name):
+    parts = lax.all_gather(x, name)
+    return jnp.sum(parts, axis=0)
 
 
 def from_partner(value, axis, apart):
@@ -92,7 +97,7 @@
         + contract_last(mask_cov_first[0], open_geno)
         + leader * contract_last(open_cov, open_geno)
     )
-    gram_share = prod_first[0] + lax.psum(partial_value, "smp")
+    gram_share = prod_first[0] + add_all(partial_value, "smp")
     weight_share = jnp.dot(coef, gram_share, precision=precise, preferred_element_type=jnp.float32)
     masked_weight = weight_share - mask_weight[0]
     peer_second, peer_weight = from_partner((masked_second, masked_weight), "srv", 0)

time: 830 us -> 344 us (0.41)
  blocking collectives: 709 us -> 29 us
  waiting for transfers between devices: 48.4 us -> 237 us
    psum x1 -> x0, blocking collectives: 674 us -> none  [local(): gram_share = prod_first[0] + lax.psum(partial_value, 'smp')]
    all_gather x0 -> x1, waiting for transfers between devices: none -> 117 us  [add_all(): parts = lax.all_gather(x, name)]
    all_gather x1, waiting for transfers between devices: 0.01 us -> 71.1 us  [local(): lax.all_gather(phenotypes, 'smp', axis=0, tiled=True)]
  transfers between devices with their start and end apart: 8 -> 9, of which waited for: 5 -> 7; matrix products, arithmetic and copies ran while one was open for 2% -> 5% of each run, Pallas kernels for 0% -> 0%
where the time goes in v1:
time: 344 us; the launch traced here: 343 us
  waiting for transfers between devices  237 us (69%)
  starting transfers between devices  29.8 us (9%)
  blocking collectives  29 us (8%)
  local copies, waits for them, and re-layouts  14.8 us (4%)
  between operations  14.5 us (4%)
  other arithmetic  9.44 us (3%)
  matrix products  7.95 us (2%)
    all_gather x1, waiting for transfers between devices, add_all(): parts = lax.all_gather(x, name)  117 us
    all_gather x1, waiting for transfers between devices, local(): lax.all_gather(phenotypes, 'smp', axis=0, tiled=True)  71.1 us
    all_to_all x1, blocking collectives, local(): lax.all_to_all(residual, 'smp', split_axis=0, concat_axis=1, tiled=True)  29 us
    all_to_all x1, waiting for transfers between devices, local(): lax.all_to_all(packed_geno, 'smp', split_axis=1, concat_axis=1, tiled=True)  27.9 us
    all_to_all x1, starting transfers between devices, local(): lax.all_to_all(placed_row, 'smp', split_axis=1, concat_axis=1, tiled=True)  15 us
    all_to_all x1, waiting for transfers between devices, local(): lax.all_to_all(packed_cov, 'smp', split_axis=1, concat_axis=1, tiled=True)  12 us
    all_to_all x1, waiting for transfers between devices, local(): lax.all_to_all(placed_row, 'smp', split_axis=1, concat_axis=1, tiled=True)  7.18 us
    all_to_all x1, starting transfers between devices, local(): lax.all_to_all(packed_cov, 'smp', split_axis=1, concat_axis=1, tiled=True)  7.07 us
  transfers between devices with their start and end apart: 9, of which 7 were waited for; matrix products, arithmetic and copies ran while one was open for 5% of the time, Pallas kernels for 0%

profile of v1, /device:TPU:32, one launch (start us, length us, event | category | flops | bytes accessed | tf_op | source)
XLA Modules:
  0.0 342.7 jit_solution(9110555417887391857)
XLA Ops:
  7.2 0.8 fusion.39
  8.1 0.1 copy.35
  8.2 0.3 fusion.15
  8.7 0.2 fusion.17
  8.9 0.7 compare_select_fusion.3
  9.6 1.4 scatter_custom_fusion.1
  11.0 1.4 scatter_custom_fusion
  12.4 1.9 gather_fusion
  14.4 0.8 all_to_all.32
  15.1 15.0 %all-to-all-start = ((f32[1,128,2]{2,0,1:T(1,128)}), f32[1,128,2]{2,0,1:T(1,128)S(1)}, u32[]{:S(2)}, u32[]{:S(2)}) async-start(f32[1,128,2]{2,0,1:T(1,128)} %bitcast.5), calls=%async_computation | async-start | bytes 131072 | tf_op jit(solution)/shard_map/all_to_all | solution.py:80
  30.3 0.3 copy.38
  30.7 1.1 gather_fusion.1
  31.7 0.6 gather.17
  32.4 0.2 broadcast_in_dim.72
  32.5 1.6 select_multiply_fusion
  34.1 7.2 %all-to-all-done = f32[1,128,2]{2,0,1:T(1,128)S(1)} async-done(((f32[1,128,2]{2,0,1:T(1,128)}), f32[1,128,2]{2,0,1:T(1,128)S(1)}, u32[]{:S(2)}, u32[]{:S(2)}) %all-to-all-start) | async-done | bytes 1056 | tf_op jit(solution)/shard_map/all_to_all | solution.py:80
  41.3 6.6 %all-to-all-start.1 = ((f32[1024,128,2]{0,2,1:T(2,128)}), f32[1024,128,2]{0,2,1:T(2,128)S(1)}, u32[]{:S(2)}, u32[]{:S(2)}) async-start(f32[1024,128,2]{0,2,1:T(2,128)} %select_multiply_fusion), calls=%async_computation.1 | async-start | bytes 2097152 | tf_op jit(solution)/shard_map/all_to_all | solution.py:78
  47.9 0.2 copy.43
  48.1 0.5 broadcast.135
  48.7 0.8 reduce.4
  49.6 27.9 %all-to-all-done.1 = f32[1024,128,2]{0,2,1:T(2,128)S(1)} async-done(((f32[1024,128,2]{0,2,1:T(2,128)}), f32[1024,128,2]{0,2,1:T(2,128)S(1)}, u32[]{:S(2)}, u32[]{:S(2)}) %all-to-all-start.1) | async-done | bytes 1048608 | tf_op jit(solution)/shard_map/all_to_all | solution.py:78
  77.5 0.7 reshape.136
  78.2 1.6 scatter_custom_fusion.2
  79.9 0.3 collective-permute-start.2
  80.3 0.7 gather_fusion.2
  81.1 1.0 select_multiply_fusion.1
  82.1 7.1 %all-to-all-start.2 = ((f32[10,128,2]{0,2,1:T(2,128)}), f32[10,128,2]{0,2,1:T(2,128)S(1)}, u32[]{:S(2)}, u32[]{:S(2)}) async-start(f32[10,128,2]{0,2,1:T(2,128)} %select_multiply_fusion.1), calls=%async_computation.2 | async-start | bytes 262144 | tf_op jit(solution)/shard_map/all_to_all | solution.py:79
  89.4 12.0 %all-to-all-done.2 = f32[10,128,2]{0,2,1:T(2,128)S(1)} async-done(((f32[10,128,2]{0,2,1:T(2,128)}), f32[10,128,2]{0,2,1:T(2,128)S(1)}, u32[]{:S(2)}, u32[]{:S(2)}) %all-to-all-start.2) | async-done | bytes 10272 | tf_op jit(solution)/shard_map/all_to_all | solution.py:79
  101.4 1.2 scatter_custom_fusion.3
  102.7 0.4 convolution_bitcast_fusion.2
  103.2 0.8 collective-permute-done.1
  104.0 0.4 convolution_multiply_fusion.1
  104.4 1.2 fusion.6
  105.6 0.7 all-gather.5.cloned.1.call-update
  106.4 117.2 %all-gather.7.cloned.1.call-done = f32[128,10,1024]{2,1,0:T(8,128)} async-done(((f32[1,10,1024]{2,1,0:T(8,128)}), f32[128,10,1024]{2,1,0:T(8,128)}) %all-gather.7.cloned.1.call-update) | async-done | bytes 5242896 | tf_op jit(solution)/shard_map/all_gather | solution.py:12
  223.6 3.9 %reduce_sum.19 = f32[10,1024]{1,0:T(8,128)S(1)} reduce(f32[128,10,1024]{2,1,0:T(8,128)} %all-gather.7.cloned.1.call-done, f32[]{:T(128)} %constant.45.clone.1), dimensions={0}, to_apply=%region_7.8 | reduce | flops 1300480 | bytes 5283844 | tf_op jit(solution)/shard_map/reduce_sum | solution.py:13
  227.5 0.2 fusion.4
  227.8 0.2 copy.39
  228.0 0.6 collective-permute-start
  228.6 0.5 collective-permute-done.3
  229.0 0.6 fusion.25
  229.6 0.6 convolution_multiply_fusion
  230.2 0.7 fusion.3
  230.9 0.2 copy.46
  231.1 29.0 %all_to_all.46 = f32[128,8,128]{2,1,0:T(8,128)S(1)} all-to-all(f32[128,8,128]{2,1,0:T(8,128)S(1)} %bitcast.89), channel_id=1, replica_groups=mesh['srv'=2,'smp'=128] {'smp'}, dimensions={0} | all-to-all | bytes 1048576 | tf_op jit(solution)/shard_map/all_to_all | solution.py:113
  260.0 71.1 %all-gather.5.cloned.1.call-done = f32[16384,32]{0,1:T(8,128)} async-done(((f32[128,32]{0,1:T(8,128)}), f32[16384,32]{0,1:T(8,128)}) %all-gather.5.cloned.1.call-update) | async-done | bytes 2097168 | tf_op jit(solution)/shard_map/all_gather | solution.py:117
  331.1 4.0 %fusion.7 = f32[1,8,32]{2,1,0:T(8,128)} fusion(f32[16384,32]{0,1:T(8,128)} %all-gather.5.cloned.1.call-done, f32[128,8,128]{2,1,0:T(8,128)S(1)} %all_to_all.46), kind=kOutput, calls=%fused_computation.21 | convolution fusion | flops 50331904 | bytes 2622464 | tf_op jit(solution)/shard_map/dot_general | solution.py:115
  335.1 0.8 copy.61
  (46 shorter events, 1.3 us)
Async XLA Ops:
  7.2 220.3 %copy-start = (f32[10,10]{1,0:T(8,128)S(1)}, f32[10,10]{1,0:T(8,128)}, u32[]{:S(2)}) copy-start(f32[10,10]{1,0:T(8,128)} %param.20) | copy-start | bytes 1204
  7.2 23.1 %copy-start.2 = (f32[1,1024,256]{2,1,0:T(8,128)S(1)}, f32[1,1024,256]{2,1,0:T(8,128)}, u32[]{:S(2)}) copy-start(f32[1,1024,256]{2,1,0:T(8,128)} %param.11) | copy-start | bytes 3145732
  15.1 26.1 %all-to-all-start = ((f32[1,128,2]{2,0,1:T(1,128)}), f32[1,128,2]{2,0,1:T(1,128)S(1)}, u32[]{:S(2)}, u32[]{:S(2)}) async-start(f32[1,128,2]{2,0,1:T(1,128)} %bitcast.5), calls=%async_computation | async-start | bytes 131072 | tf_op jit(solution)/shard_map/all_to_all | solution.py:80
  32.5 15.4 %copy-start.1 = (f32[1,1024,128]{2,1,0:T(8,128)S(1)}, f32[1,1024,128]{2,1,0:T(8,128)}, u32[]{:S(2)}) copy-start(f32[1,1024,128]{2,1,0:T(8,128)} %param.15) | copy-start | bytes 1572868
  41.3 36.2 %all-to-all-start.1 = ((f32[1024,128,2]{0,2,1:T(2,128)}), f32[1024,128,2]{0,2,1:T(2,128)S(1)}, u32[]{:S(2)}, u32[]{:S(2)}) async-start(f32[1024,128,2]{0,2,1:T(2,128)} %select_multiply_fusion), calls=%async_computation.1 | async-start | bytes 2097152 | tf_op jit(solution)/shard_map/all_to_all | solution.py:78
  78.2 2.0 copy-start.6
  78.2 11.0 %copy-start.7 = (f32[1,10,128]{2,0,1:T(1,128)S(1)}, f32[1,10,128]{2,0,1:T(1,128)}, u32[]{:S(2)}) copy-start(f32[1,10,128]{2,0,1:T(1,128)} %param.14) | copy-start | bytes 15364
  78.2 11.1 %copy-start.8 = (f32[1,10,128]{2,0,1:T(1,128)S(1)}, f32[1,10,128]{2,0,1:T(1,128)}, u32[]{:S(2)}) copy-start(f32[1,10,128]{2,0,1:T(1,128)} %param.17) | copy-start | bytes 15364
  79.9 22.8 %collective-permute-start.2 = (f32[1024,128]{0,1:T(8,128)S(1)}, f32[1024,128]{0,1:T(8,128)S(1)}, u32[]{:S(2)}, u32[]{:S(2)}) collective-permute-start(f32[1024,128]{0,1:T(8,128)S(1)} %bitcast_subtract_fusion), channel_id=1, source_target_pairs={{0,128},{128,0},{1,129},{129,1},{2,130},{130,2},{3,131},{131,3},{4... | collective-permute-start | bytes 1572872 | tf_op jit(solution)/shard_map/ppermute | solution.py:19
  82.1 19.4 %all-to-all-start.2 = ((f32[10,128,2]{0,2,1:T(2,128)}), f32[10,128,2]{0,2,1:T(2,128)S(1)}, u32[]{:S(2)}, u32[]{:S(2)}) async-start(f32[10,128,2]{0,2,1:T(2,128)} %select_multiply_fusion.1), calls=%async_computation.2 | async-start | bytes 262144 | tf_op jit(solution)/shard_map/all_to_all | solution.py:79
  89.1 134.4 %all-gather.7.cloned.1.call-start = ((), (), s32[]{:S(2)}) async-start(), calls=%async_computation.5 | async-start | bytes 8454144 | tf_op jit(solution)/shard_map/all_gather | solution.py:12
  102.6 1.3 collective-permute-start.1
  105.6 225.5 %all-gather.5.cloned.1.call-start = ((), (), s32[]{:S(2)}) async-start(), calls=%async_computation.4 | async-start | bytes 2113536 | tf_op jit(solution)/shard_map/all_gather | solution.py:117
  106.4 121.1 %copy-start.4 = (f32[1,10,1024]{2,0,1:T(1,128)S(1)}, f32[1,10,1024]{2,0,1:T(1,128)}, u32[]{:S(2)}) copy-start(f32[1,10,1024]{2,0,1:T(1,128)} %param.18) | copy-start | bytes 122884
  106.4 121.1 %copy-start.5 = (f32[1,10,1024]{2,0,1:T(1,128)S(1)}, f32[1,10,1024]{2,0,1:T(1,128)}, u32[]{:S(2)}) copy-start(f32[1,10,1024]{2,0,1:T(1,128)} %param.16) | copy-start | bytes 122884
  106.4 121.4 %copy-start.3 = (f32[1,1024,128]{2,1,0:T(8,128)S(1)}, f32[1,1024,128]{2,1,0:T(8,128)}, u32[]{:S(2)}) copy-start(f32[1,1024,128]{2,1,0:T(8,128)} %param.19) | copy-start | bytes 1572868
  227.7 1.3 collective-permute-start.3
  228.0 1.6 collective-permute-start
Sparse Core Ops, SparseCore 0:
  105.7 117.7 all-gather.6
  227.0 104.0 all-gather.4
